TPU v7x, 128 devices: a whole 4x4x4 slice. The times are simulated.
128 devices in a mesh: row: 4 (over x), col: 8 (over z_lo, y), layer: 4 (over z_hi, core).
Axes of the slice: x: 4, y: 4, z: 4 (z_hi: 2, z_lo: 2; z = z_hi * 2 + z_lo), core: 2. Of those that a mesh axis runs over, the one named last changes fastest.
Arguments:
- a_blocks: float32 [4096, 4096], P('row', ('col', 'layer')), may hold values from -6 to 6
- mask_a: int32 [64, 64], P('row', ('col', 'layer')), may hold values from 0 to 1, as said below
- b_blocks: float32 [4096, 32768], P('row', ('col', 'layer')), may hold values from -0.25 to 0.25
- mask_b: int32 [64, 512], P('row', ('col', 'layer')), may hold values from 0 to 1
Outputs:
- product: float32 [4096, 32768], P('row', ('col', 'layer'))
Inputs may be any that keep to these rules, and one draw needn't show every extreme that they name: Within one device's shard of mask_a (16 block rows by 2 inner block indices) at most 8 blocks are stored; the shard of the first 16 block rows and first 2 inner indices stores exactly 8.
All inputs are finite; a program needn't handle non-finite values.
Results may differ from a plain program's by a relative error of at most 0.00007.
Values sent between devices are 32-bit elements; how exact they have to be, the bound alone decides.
No kernel may reach another device: no remote copies, remote signals or barrier semaphores. Data moves between devices by JAX's collectives and lax.ppermute only.
A program may use at most 128 MiB of HBM per device.

v0:
```python
import jax
import jax.numpy as jnp
from jax import lax
from jax.sharding import PartitionSpec as P

BLOCK = 64


def expand(mask):
    return jnp.repeat(jnp.repeat(mask, BLOCK, axis=0), BLOCK, axis=1).astype(jnp.float32)


def shards(a_blocks, mask_a, b_blocks, mask_b):
    b_masked = b_blocks * expand(mask_b)
    b_whole = lax.all_gather(b_masked, "row", axis=0, tiled=True)
    a_masked = a_blocks * expand(mask_a)
    return jnp.dot(
        lax.all_gather(a_masked, ("col", "layer"), axis=1, tiled=True),
        b_whole,
        precision=lax.Precision.HIGHEST,
        preferred_element_type=jnp.float32,
    )


def solution(mesh):
    placed = (
        P("row", ("col", "layer")),
        P("row", ("col", "layer")),
        P("row", ("col", "layer")),
        P("row", ("col", "layer")),
    )
    return jax.shard_map(
        shards, mesh=mesh, in_specs=placed, out_specs=P("row", ("col", "layer")), check_vma=False
    )
```

profile of v0, /device:TPU:1, one launch (start us, length us, event | category | flops | bytes accessed | tf_op | source)
XLA Modules:
  0.0 392.4 jit_solution(702926884030204920)
XLA Ops:
  6.5 0.0 copy-start
  6.5 0.0 copy-start.1
  6.5 0.0 all-gather.5.cloned.1.call-start
  6.5 5.4 %copy.8 = f32[1024,1024]{0,1:T(8,128)} copy(f32[1024,1024]{1,0:T(8,128)} %param.6) | data formatting | bytes 8388608 | tf_op args[2]
  11.9 0.7 convert_element_type.25
  12.6 0.1 copy.7
  12.7 0.1 broadcast_in_dim.14
  12.8 0.1 convert_element_type.26
  12.9 5.1 %bitcast_multiply_fusion = f32[1024,1024]{0,1:T(8,128)} fusion(f32[1024,1024]{0,1:T(8,128)} %copy.8, f32[1024,16]{0,1:T(8,128)S(1)} %convert_element_type.26), kind=kLoop, calls=%fused_computation | loop fusion | flops 1048576 | bytes 8454144 | tf_op jit(solution)/shard_map/mul | solution.py:14
  18.0 0.0 all-gather.5.cloned.1.call-update
  18.0 0.0 all-gather.3.cloned.1.call-start
  18.0 0.0 copy-done
  18.1 0.2 copy.6
  18.3 0.0 copy-done.1
  18.3 0.1 broadcast_in_dim.12
  18.4 0.1 convert_element_type.23
  18.4 0.9 bitcast_multiply_fusion.1
  19.3 0.0 all-gather.3.cloned.1.call-update
  19.3 156.1 %all-gather.5.cloned.1.call-done = f32[4096,1024]{0,1:T(8,128)} async-done(((f32[1024,1024]{0,1:T(8,128)}), f32[4096,1024]{0,1:T(8,128)}) %all-gather.5.cloned.1.call-update) | async-done | bytes 16777232 | tf_op jit(solution)/shard_map/all_gather | solution.py:15
  175.4 100.4 %all-gather.3.cloned.1.call-done = f32[1024,4096]{0,1:T(8,128)} async-done(((f32[1024,128]{0,1:T(8,128)}), f32[1024,4096]{0,1:T(8,128)}) %all-gather.3.cloned.1.call-update) | async-done | bytes 16777232 | tf_op jit(solution)/shard_map/all_gather | solution.py:18
  275.8 109.8 %fusion = f32[1024,1024]{1,0:T(8,128)} fusion(f32[1024,4096]{0,1:T(8,128)} %all-gather.3.cloned.1.call-done, f32[4096,1024]{0,1:T(8,128)} %all-gather.5.cloned.1.call-done), kind=kOutput, calls=%fused_computation.2 | convolution fusion | flops 51539607552 | bytes 37748736 | tf_op jit(solution)/shard_map/dot_general | solution.py:17
  (1 shorter events, 0.0 us)
Async XLA Ops:
  6.5 11.5 %copy-start = (f32[1024,128]{1,0:T(8,128)S(1)}, f32[1024,128]{1,0:T(8,128)}, u32[]{:S(2)}) copy-start(f32[1024,128]{1,0:T(8,128)} %param.4) | copy-start | bytes 1572868
  6.5 11.7 %copy-start.1 = (s32[16,2]{0,1:T(2,128)S(1)}, s32[16,2]{0,1:T(2,128)}, u32[]{:S(2)}) copy-start(s32[16,2]{0,1:T(2,128)} %param.5) | copy-start | bytes 388
  6.5 168.9 %all-gather.5.cloned.1.call-start = ((), (), s32[]{:S(2)}) async-start(), calls=%async_computation.1 | async-start | bytes 20971520 | tf_op jit(solution)/shard_map/all_gather | solution.py:15
  18.0 257.8 %all-gather.3.cloned.1.call-start = ((), (), s32[]{:S(2)}) async-start(), calls=%async_computation | async-start | bytes 17301504 | tf_op jit(solution)/shard_map/all_gather | solution.py:18
Sparse Core Ops, SparseCore 0:
  18.1 157.2 all-gather.4
  177.1 98.6 all-gather.2
where the time goes:
time: 393 us; the launch traced here: 392 us
  waiting for transfers between devices  256 us (65%)
  matrix products  110 us (28%)
  between operations  13.4 us (3%)
  other arithmetic  6.62 us (2%)
  local copies, waits for them, and re-layouts  6.02 us (2%)
    all_gather x1, waiting for transfers between devices, shards(): b_whole = lax.all_gather(b_masked, 'row', axis=0, tiled=True)  156 us
    dot_general x1, matrix products, shards(): jnp.dot(lax.all_gather(a_masked, ('col', 'layer'), axis=1, tiled=True), b...  110 us
    all_gather x1, waiting for transfers between devices, shards(): lax.all_gather(a_masked, ('col', 'layer'), axis=1, tiled=True)  100 us
  transfers between devices with their start and end apart: 2, of which 2 were waited for; matrix products, arithmetic and copies ran while one was open for 0% of the time, Pallas kernels for 0%

commit v1 on v0

--- a/solution.py
+++ b/solution.py
@@ -2,6 +2,7 @@
 import jax.numpy as jnp
 from jax import lax
 from jax.sharding import PartitionSpec as P
+from jax.lax import all_to_all, axis_size
 
 BLOCK = 64
 
@@ -12,7 +13,15 @@
 
 def shards(a_blocks, mask_a, b_blocks, mask_b):
     b_masked = b_blocks * expand(mask_b)
-    b_whole = lax.all_gather(b_masked, "row", axis=0, tiled=True)
+    b_whole = jnp.concatenate(
+        all_to_all(
+            jnp.stack([b_masked for _ in range(axis_size("row"))]),
+            axis_name="row",
+            split_axis=0,
+            concat_axis=0,
+        ),
+        0,
+    )
     a_masked = a_blocks * expand(mask_a)
     return jnp.dot(
         lax.all_gather(a_masked, ("col", "layer"), axis=1, tiled=True),

time: 393 us -> 299 us (0.76)
  waiting for transfers between devices: 256 us -> 0.02 us
  blocking collectives: 0 us -> 195 us
  matrix products: 110 us -> 59.5 us
  local copies, waits for them, and re-layouts: 6.02 us -> 23 us
    all_to_all x0 -> x1, blocking collectives: none -> 195 us  [shards(): all_to_all(jnp.stack([b_masked for _ in range(axis_size('row'))]), axis_n...]
    all_gather x1 -> x0, waiting for transfers between devices: 156 us -> none  [shards(): b_whole = lax.all_gather(b_masked, 'row', axis=0, tiled=True)]
    all_gather x1, waiting for transfers between devices: 100 us -> 0.01 us  [shards(): lax.all_gather(a_masked, ('col', 'layer'), axis=1, tiled=True)]
    dot_general x1, matrix products: 110 us -> 59.5 us  [shards(): jnp.dot(lax.all_gather(a_masked, ('col', 'layer'), axis=1, tiled=True), b...]
    another operation x0 -> x1, local copies, waits for them, and re-layouts: none -> 10.6 us  [shards(): jnp.stack([b_masked for _ in range(axis_size('row'))])]
    mul x0 -> x1, local copies, waits for them, and re-layouts: none -> 5.42 us  [shards(): b_masked = b_blocks * expand(mask_b)]
  transfers between devices with their start and end apart: 2 -> 1, of which waited for: 2 -> 0; matrix products, arithmetic and copies ran while one was open for 0% -> 9% of each run, Pallas kernels for 0% -> 0%
where the time goes in v1:
time: 299 us
  blocking collectives  195 us (65%)
  matrix products  59.5 us (20%)
  local copies, waits for them, and re-layouts  23 us (8%)
  between operations  13.4 us (4%)
  other arithmetic  7.3 us (2%)
    all_to_all x1, blocking collectives, shards(): all_to_all(jnp.stack([b_masked for _ in range(axis_size('row'))]), axis_n...  195 us
    dot_general x1, matrix products, shards(): jnp.dot(lax.all_gather(a_masked, ('col', 'layer'), axis=1, tiled=True), b...  59.5 us
    another operation x1, local copies, waits for them, and re-layouts, shards(): jnp.stack([b_masked for _ in range(axis_size('row'))])  10.6 us
    unnamed x2, local copies, waits for them, and re-layouts  6.58 us
  transfers between devices with their start and end apart: 1, of which 0 were waited for; matrix products, arithmetic and copies ran while one was open for 9% of the time, Pallas kernels for 0%

profile of v1, /device:TPU:1, one launch (start us, length us, event | category | flops | bytes accessed | tf_op | source)
XLA Modules:
  0.0 298.6 jit_solution(2731565274236527439)
XLA Ops:
  6.5 0.0 all-gather.2.cloned.1.call-start
  6.5 1.2 copy.6
  7.8 0.7 convert_element_type.22
  8.5 0.1 broadcast_in_dim.12
  8.5 0.1 convert_element_type.23
  8.6 0.9 bitcast_multiply_fusion.1
  9.5 0.0 all-gather.2.cloned.1.call-update
  9.5 5.3 %copy.8 = f32[1024,1024]{0,1:T(8,128)} copy(f32[1024,1024]{1,0:T(8,128)} %param.6) | data formatting | bytes 8388608 | tf_op args[2]
  14.9 0.7 convert_element_type.25
  15.5 0.1 copy.7
  15.6 0.1 broadcast_in_dim.14
  15.7 0.1 convert_element_type.26
  15.8 5.1 %bitcast_multiply_fusion = f32[1024,1024]{0,1:T(8,128)} fusion(f32[1024,1024]{0,1:T(8,128)} %copy.8, f32[1024,16]{0,1:T(8,128)S(1)} %convert_element_type.26), kind=kLoop, calls=%fused_computation | loop fusion | flops 1048576 | bytes 8454144 | tf_op jit(solution)/shard_map/mul | solution.py:15
  20.9 5.4 %copy.9 = f32[1024,1024]{1,0:T(8,128)} copy(f32[1024,1024]{0,1:T(8,128)} %bitcast_multiply_fusion) | data formatting | bytes 8388608 | tf_op jit(solution)/shard_map/mul | solution.py:15
  26.3 10.6 %stack.2 = f32[4,1024,1024]{2,1,0:T(8,128)} broadcast(f32[1024,1024]{1,0:T(8,128)} %copy.9), dimensions={1,2} | broadcast | bytes 20971520 | tf_op jit(solution)/shard_map/stack | solution.py:18
  36.9 195.3 %all_to_all.5 = f32[4,1024,1024]{2,1,0:T(8,128)} all-to-all(f32[4,1024,1024]{2,1,0:T(8,128)} %stack.2), channel_id=1, replica_groups=mesh['row'=4,'col'=8,'layer'=4] {'row'}, dimensions={0} | all-to-all | bytes 33554432 | tf_op jit(solution)/shard_map/all_to_all | solution.py:17
  232.2 0.0 all-gather.2.cloned.1.call-done
  232.3 59.5 %fusion = f32[1024,1024]{1,0:T(8,128)} fusion(f32[1024,4096]{0,1:T(8,128)} %all-gather.2.cloned.1.call-done, f32[4096,1024]{1,0:T(8,128)} %bitcast.11), kind=kOutput, calls=%fused_computation.2 | convolution fusion | flops 51539607552 | bytes 37748736 | tf_op jit(solution)/shard_map/dot_general | solution.py:26
Async XLA Ops:
  6.5 225.7 %all-gather.2.cloned.1.call-start = ((), (), s32[]{:S(2)}) async-start(), calls=%async_computation.1 | async-start | bytes 17301504 | tf_op jit(solution)/shard_map/all_gather | solution.py:27
Sparse Core Ops, SparseCore 0:
  9.6 100.8 all-gather.1
